TPU v7x, 32 devices: a whole 2x2x4 slice. The times are simulated.
32 devices in a mesh: member: 8 (over z, core), dp: 4 (over y, x).
Axes of the slice: x: 2, y: 2, z: 4, core: 2. Of those that a mesh axis runs over, the one named last changes fastest.
Arguments:
- feats: bfloat16 [8, 2048, 1024], P('member', 'dp'), may hold values from -160 to 160
- pair_weight: float32 [8, 3], replicated, may hold values from 0.5 to 2
Outputs:
- grad_centred: float32 [8, 2048, 1024], P('member', 'dp')
- cka: float32 [8, 3], P('member')
All inputs are finite; a program needn't handle non-finite values.
Results may differ from a plain program's by a relative error of at most 0.0053.
Values may be sent and summed in bfloat16 or wider, within the bound.
A program may use at most 128 MiB of HBM per device.

v0:
```python
import math
import jax
import jax.numpy as jnp
from jax import lax
from jax.sharding import PartitionSpec as P


def mixing(self_hsic, pair_hsic, pair_weight):
    pairs = pair_weight.shape[1]
    members = pair_weight.shape[0]
    partner_self = jnp.stack([jnp.roll(self_hsic, -o) for o in range(1, pairs + 1)], axis=1)
    norms = jnp.sqrt(self_hsic[:, None] * partner_self)
    cka = pair_hsic / norms
    weighted = pair_weight * cka
    incoming = sum((jnp.roll(weighted[:, o - 1], o) for o in range(1, pairs + 1)))
    self_coef = (jnp.sum(weighted, axis=1) + incoming) / (self_hsic + 1e-06)
    coef = 2.0 * pair_weight / norms
    eye = jnp.eye(members, dtype=jnp.float32)
    mix = -2.0 * self_coef[:, None] * eye
    for o in range(1, pairs + 1):
        ahead = coef[:, o - 1][:, None] * jnp.roll(eye, o, axis=1)
        mix = mix + ahead + ahead.T
    return (cka, mix)


def shards(feats, pair_weight):
    rows = feats[0]
    members = lax.axis_size("member")
    pairs = pair_weight.shape[1]
    whole = lax.all_gather(rows, "dp", axis=0, tiled=True)
    batch, width = whole.shape
    mean = jnp.sum(whole.astype(jnp.float32), axis=0) / batch
    centred = (whole.astype(jnp.float32) - mean).astype(jnp.bfloat16)
    own = (rows.astype(jnp.float32) - mean).astype(jnp.bfloat16)
    blocks = centred.reshape(members, batch // members, width)
    gram = jnp.einsum("rf,mcf->mrc", own, blocks, preferred_element_type=jnp.float32)
    held = lax.all_to_all(gram.astype(jnp.bfloat16), "member", 0, 0)
    held = held.astype(jnp.float32)
    sums = []
    for o in range(pairs + 1):
        sums.append(jnp.sum(held * jnp.roll(held, -o, axis=0), axis=(1, 2)))
    sums = lax.psum(jnp.stack(sums, axis=1), ("member", "dp"))
    cka, mix = mixing(sums[:, 0], sums[:, 1:], pair_weight)
    mixed = jnp.stack(
        [sum((mix[m, q] * held[q] for q in range(members))) for m in range(members)]
    ).astype(jnp.bfloat16)
    mixed = lax.all_to_all(mixed, "member", 0, 0)
    grad = jnp.einsum("jrc,jcf->rf", mixed, blocks, preferred_element_type=jnp.float32)
    grad = math.sqrt(batch) * grad
    own_cka = lax.dynamic_slice_in_dim(cka, lax.axis_index("member"), 1, axis=0)
    return (grad[None], own_cka)


def solution(mesh):
    return jax.shard_map(
        shards,
        mesh=mesh,
        in_specs=(P("member", "dp", None), P()),
        out_specs=(P("member", "dp", None), P("member", None)),
        check_vma=False,
    )
```

profile of v0, /device:TPU:0, one launch (start us, length us, event | category | flops | bytes accessed | tf_op | source)
XLA Modules:
  0.0 292.4 jit_solution(5384150362921916437)
XLA Ops:
  7.9 57.2 %all-gather.3.cloned.1.call-done = bf16[1,2048,1024]{2,1,0:T(8,128)(2,1)} async-done(((bf16[1,512,1024]{2,1,0:T(8,128)(2,1)}), bf16[1,2048,1024]{2,1,0:T(8,128)(2,1)}) %all-gather.3.cloned.1.call-update) | async-done | bytes 4194320 | tf_op jit(solution)/shard_map/all_gather | solution.py:30
  65.1 3.0 %convert_reduce_fusion = f32[1024]{0:T(1024)S(1)} fusion(bf16[1,2048,1024]{2,1,0:T(8,128)(2,1)} %all-gather.3.cloned.1.call-done), kind=kLoop, calls=%fused_computation | loop fusion | flops 4193280 | bytes 4198400 | tf_op jit(solution)/shard_map/reduce_sum | solution.py:32
  68.6 1.3 fusion.1
  69.9 1.9 copy-done
  71.8 3.8 %convert_bitcast_fusion.1 = bf16[8,512,256]{1,2,0:T(8,128)(2,1)} fusion(bf16[8,256,1024]{2,1,0:T(8,128)(2,1)S(1)} %bitcast.136, bf16[1,512,1024]{2,1,0:T(8,128)(2,1)S(1)} %copy-done.2, f32[1024]{0:T(1024)S(1)} %broadcast_multiply_fusion), kind=kOutput, calls=%fused_computation.13 | convolution fusion | flops 2150105088 | bytes 7344128 | tf_op jit(solution)/shard_map/rf,mcf->mrc/dot_general | solution.py:36
  75.5 4.6 %all-to-all-start = ((bf16[8,512,256]{1,2,0:T(8,128)(2,1)}), bf16[8,512,256]{1,2,0:T(8,128)(2,1)S(1)}, u32[]{:S(2)}, u32[]{:S(2)}) async-start(bf16[8,512,256]{1,2,0:T(8,128)(2,1)} %convert_bitcast_fusion.1), calls=%async_computation | async-start | bytes 4194304 | tf_op jit(solution)/shard_map/all_to_all | solution.py:37
  80.5 48.6 %all-to-all-done = bf16[8,512,256]{1,2,0:T(8,128)(2,1)S(1)} async-done(((bf16[8,512,256]{1,2,0:T(8,128)(2,1)}), bf16[8,512,256]{1,2,0:T(8,128)(2,1)S(1)}, u32[]{:S(2)}, u32[]{:S(2)}) %all-to-all-start) | async-done | bytes 2097184 | tf_op jit(solution)/shard_map/all_to_all | solution.py:37
  130.9 1.8 multiply_reduce_fusion
  132.8 37.0 %psum.7 = f32[8,4]{0,1:T(4,128)S(1)} all-reduce(f32[8,4]{0,1:T(4,128)S(1)} %pad_maximum_fusion), channel_id=1, replica_groups=mesh['member'=8,'dp'=4] {'member','dp'}, use_global_device_ids=true, to_apply=%region_5.6 | all-reduce | flops 32 | bytes 256 | tf_op jit(solution)/shard_map/psum | solution.py:42
  170.5 0.7 maximum_bitcast_fusion
  172.2 0.7 slice_bitcast_fusion.1
  173.3 0.7 fusion.26
  175.4 0.7 fusion.24
  176.7 6.4 %fusion.9 = bf16[8,512,256]{1,2,0:T(8,128)(2,1)} fusion(f32[8,512,256]{1,2,0:T(8,128)S(1)} %convert_element_type.47, f32[]{:T(128)} %bitcast.34, f32[]{:T(128)} %bitcast.33, f32[]{:T(128)} %bitcast.32, f32[]{:T(128)} %bitcast.31, f32[]{:T(128)} %bitcast.30, f32[]{:T(128)} %bitcast.29, f32[]{:T(128)} %bitcast.28, f32[]{:T(128)} %bitcast.27), kind=kLoop, calls=%fused_computation.25 | loop fusion | flops 2097151 | bytes 4456480
  183.1 6.1 %fusion.10 = bf16[8,512,256]{1,2,0:T(8,128)(2,1)} fusion(bf16[8,512,256]{1,2,0:T(8,128)(2,1)} %fusion.9, f32[8,512,256]{1,2,0:T(8,128)S(1)} %convert_element_type.47, f32[]{:T(128)} %bitcast.42, f32[]{:T(128)} %bitcast.41, f32[]{:T(128)} %bitcast.40, f32[]{:T(128)} %bitcast.39, f32[]{:T(128)} %bitcast.38, f32[]{:T(128)} %bitcast.37, f32[]{:T(128)} %bitcast.36, ...), kind=kLoop, calls=%fused_computation.26 | loop fusion | flops 2097152 | bytes 4460544
  189.2 6.1 %fusion.11 = bf16[8,512,256]{1,2,0:T(8,128)(2,1)} fusion(bf16[8,512,256]{1,2,0:T(8,128)(2,1)} %fusion.10, f32[8,512,256]{1,2,0:T(8,128)S(1)} %convert_element_type.47, f32[]{:T(128)} %bitcast.50, f32[]{:T(128)} %bitcast.49, f32[]{:T(128)} %bitcast.48, f32[]{:T(128)} %bitcast.47, f32[]{:T(128)} %bitcast.46, f32[]{:T(128)} %bitcast.45, f32[]{:T(128)} %bitcast.44, ...), kind=kLoop, calls=%fused_computation.27 | loop fusion | flops 2097152 | bytes 4460544
  195.3 6.1 %fusion.12 = bf16[8,512,256]{1,2,0:T(8,128)(2,1)} fusion(bf16[8,512,256]{1,2,0:T(8,128)(2,1)} %fusion.11, f32[8,512,256]{1,2,0:T(8,128)S(1)} %convert_element_type.47, f32[]{:T(128)} %bitcast.58, f32[]{:T(128)} %bitcast.57, f32[]{:T(128)} %bitcast.56, f32[]{:T(128)} %bitcast.55, f32[]{:T(128)} %bitcast.54, f32[]{:T(128)} %bitcast.53, f32[]{:T(128)} %bitcast.52, ...), kind=kLoop, calls=%fused_computation.28 | loop fusion | flops 2097152 | bytes 4460544
  201.4 6.3 %fusion.13 = bf16[8,512,256]{1,2,0:T(8,128)(2,1)} fusion(bf16[8,512,256]{1,2,0:T(8,128)(2,1)} %fusion.12, f32[8,512,256]{1,2,0:T(8,128)S(1)} %convert_element_type.47, f32[]{:T(128)} %bitcast.66, f32[]{:T(128)} %bitcast.65, f32[]{:T(128)} %bitcast.64, f32[]{:T(128)} %bitcast.63, f32[]{:T(128)} %bitcast.62, f32[]{:T(128)} %bitcast.61, f32[]{:T(128)} %bitcast.60, ...), kind=kLoop, calls=%fused_computation.29 | loop fusion | flops 2097152 | bytes 4460544
  207.7 6.2 %fusion.14 = bf16[8,512,256]{1,2,0:T(8,128)(2,1)} fusion(bf16[8,512,256]{1,2,0:T(8,128)(2,1)} %fusion.13, f32[8,512,256]{1,2,0:T(8,128)S(1)} %convert_element_type.47, f32[]{:T(128)} %bitcast.74, f32[]{:T(128)} %bitcast.73, f32[]{:T(128)} %bitcast.72, f32[]{:T(128)} %bitcast.71, f32[]{:T(128)} %bitcast.70, f32[]{:T(128)} %bitcast.69, f32[]{:T(128)} %bitcast.68, ...), kind=kLoop, calls=%fused_computation.30 | loop fusion | flops 2097152 | bytes 4460544
  214.0 6.2 %fusion.15 = bf16[8,512,256]{1,2,0:T(8,128)(2,1)} fusion(bf16[8,512,256]{1,2,0:T(8,128)(2,1)} %fusion.14, f32[8,512,256]{1,2,0:T(8,128)S(1)} %convert_element_type.47, f32[]{:T(128)} %bitcast.82, f32[]{:T(128)} %bitcast.81, f32[]{:T(128)} %bitcast.80, f32[]{:T(128)} %bitcast.79, f32[]{:T(128)} %bitcast.78, f32[]{:T(128)} %bitcast.77, f32[]{:T(128)} %bitcast.76, ...), kind=kLoop, calls=%fused_computation.31 | loop fusion | flops 2097152 | bytes 4460544
  220.2 6.2 %fusion.16 = bf16[8,512,256]{1,2,0:T(8,128)(2,1)} fusion(bf16[8,512,256]{1,2,0:T(8,128)(2,1)} %fusion.15, f32[8,512,256]{1,2,0:T(8,128)S(1)} %convert_element_type.47, f32[]{:T(128)} %bitcast.90, f32[]{:T(128)} %bitcast.89, f32[]{:T(128)} %bitcast.88, f32[]{:T(128)} %bitcast.87, f32[]{:T(128)} %bitcast.86, f32[]{:T(128)} %bitcast.85, f32[]{:T(128)} %bitcast.84, ...), kind=kLoop, calls=%fused_computation.32 | loop fusion | flops 2097152 | bytes 4460544 | tf_op jit(solution)/shard_map/stack | solution.py:44
  226.4 4.2 %all-to-all-start.1 = ((bf16[8,512,256]{1,2,0:T(8,128)(2,1)}), bf16[8,512,256]{1,2,0:T(8,128)(2,1)S(1)}, u32[]{:S(2)}, u32[]{:S(2)}) async-start(bf16[8,512,256]{1,2,0:T(8,128)(2,1)} %fusion.16), calls=%async_computation.1 | async-start | bytes 4194304 | tf_op jit(solution)/shard_map/all_to_all | solution.py:47
  231.3 48.4 %all-to-all-done.1 = bf16[8,512,256]{1,2,0:T(8,128)(2,1)S(1)} async-done(((bf16[8,512,256]{1,2,0:T(8,128)(2,1)}), bf16[8,512,256]{1,2,0:T(8,128)(2,1)S(1)}, u32[]{:S(2)}, u32[]{:S(2)}) %all-to-all-start.1) | async-done | bytes 2097184 | tf_op jit(solution)/shard_map/all_to_all | solution.py:47
  279.7 5.9 %fusion.5 = f32[1,512,1024]{2,1,0:T(8,128)} fusion(bf16[8,512,256]{1,2,0:T(8,128)(2,1)S(1)} %all-to-all-done.1, bf16[8,256,1024]{2,1,0:T(8,128)(2,1)} %bitcast.137), kind=kOutput, calls=%fused_computation.12 | convolution fusion | flops 2148007936 | bytes 8388608 | tf_op jit(solution)/shard_map/jrc,jcf->rf/dot_general | solution.py:48
  (53 shorter events, 8.0 us)
Async XLA Ops:
  7.2 58.0 %all-gather.3.cloned.1.call-start = ((), (), s32[]{:S(2)}) async-start(), calls=%async_computation.2 | async-start | bytes 5242880 | tf_op jit(solution)/shard_map/all_gather | solution.py:30
  65.1 3.4 %copy-start.1 = (bf16[1,2048,1024]{2,1,0:T(8,128)(2,1)S(1)}, bf16[1,2048,1024]{2,1,0:T(8,128)(2,1)}, u32[]{:S(2)}) copy-start(bf16[1,2048,1024]{2,1,0:T(8,128)(2,1)} %all-gather.3.cloned.1.call-done) | copy-start | bytes 12582916
  68.6 3.2 %copy-start.2 = (bf16[1,512,1024]{2,1,0:T(8,128)(2,1)S(1)}, bf16[1,512,1024]{2,1,0:T(8,128)(2,1)}, u32[]{:S(2)}) copy-start(bf16[1,512,1024]{2,1,0:T(8,128)(2,1)} %param.2) | copy-start | bytes 3145732
  69.9 1.9 copy-start
  75.5 53.6 %all-to-all-start = ((bf16[8,512,256]{1,2,0:T(8,128)(2,1)}), bf16[8,512,256]{1,2,0:T(8,128)(2,1)S(1)}, u32[]{:S(2)}, u32[]{:S(2)}) async-start(bf16[8,512,256]{1,2,0:T(8,128)(2,1)} %convert_bitcast_fusion.1), calls=%async_computation | async-start | bytes 4194304 | tf_op jit(solution)/shard_map/all_to_all | solution.py:37
  130.9 40.5 %copy-start.3 = (f32[8,3]{0,1:T(4,128)S(1)}, f32[8,3]{0,1:T(4,128)}, u32[]{:S(2)}) copy-start(f32[8,3]{0,1:T(4,128)} %param.3) | copy-start | bytes 292
  226.4 53.3 %all-to-all-start.1 = ((bf16[8,512,256]{1,2,0:T(8,128)(2,1)}), bf16[8,512,256]{1,2,0:T(8,128)(2,1)S(1)}, u32[]{:S(2)}, u32[]{:S(2)}) async-start(bf16[8,512,256]{1,2,0:T(8,128)(2,1)} %fusion.16), calls=%async_computation.1 | async-start | bytes 4194304 | tf_op jit(solution)/shard_map/all_to_all | solution.py:47
Sparse Core Ops, SparseCore 0:
  9.8 55.2 all-gather.2
where the time goes:
time: 293 us; the launch traced here: 292 us
  waiting for transfers between devices  155 us (53%)
  other arithmetic  58.2 us (20%)
  blocking collectives  37 us (13%)
  between operations  14.1 us (5%)
  local copies, waits for them, and re-layouts  9.6 us (3%)
  matrix products  9.6 us (3%)
  starting transfers between devices  8.86 us (3%)
    all_gather x1, waiting for transfers between devices, shards(): whole = lax.all_gather(rows, 'dp', axis=0, tiled=True)  57.2 us
    all_to_all x1, waiting for transfers between devices, shards(): held = lax.all_to_all(gram.astype(jnp.bfloat16), 'member', 0, 0)  48.6 us
    all_to_all x1, waiting for transfers between devices, shards(): mixed = lax.all_to_all(mixed, 'member', 0, 0)  48.4 us
    unnamed x7, other arithmetic  43.5 us
    psum x1, blocking collectives, shards(): sums = lax.psum(jnp.stack(sums, axis=1), ('member', 'dp'))  37 us
    another operation x1, other arithmetic, shards(): jnp.stack([sum((mix[m, q] * held[q] for q in range(members))) for m in ra...  6.23 us
  transfers between devices with their start and end apart: 3, of which 3 were waited for; matrix products, arithmetic and copies ran while one was open for 0% of the time, Pallas kernels for 0%

commit v1 on v0

--- a/solution.py
+++ b/solution.py
@@ -27,7 +27,12 @@
     rows = feats[0]
     members = lax.axis_size("member")
     pairs = pair_weight.shape[1]
-    whole = lax.all_gather(rows, "dp", axis=0, tiled=True)
+    ring = [rows]
+    for hop in range(3):
+        ring.append(lax.ppermute(ring[-1], "dp", [(dev, (dev + 1) % 4) for dev in range(4)]))
+    whole = jnp.roll(
+        jnp.concatenate(ring[::-1], axis=0), (lax.axis_index("dp") + 1) * ring[0].shape[0], axis=0
+    )
     batch, width = whole.shape
     mean = jnp.sum(whole.astype(jnp.float32), axis=0) / batch
     centred = (whole.astype(jnp.float32) - mean).astype(jnp.bfloat16)

time: 293 us -> 299 us (1.020)
  waiting for transfers between devices: 155 us -> 170 us
  between operations: 14.1 us -> 0.82 us
  starting transfers between devices: 8.86 us -> 12.5 us
    ppermute x0 -> x3, waiting for transfers between devices: none -> 73.2 us  [shards(): lax.ppermute(ring[-1], 'dp', [(dev, (dev + 1) % 4) for dev in range(4)])]
    all_gather x1 -> x0, waiting for transfers between devices: 57.2 us -> none  [shards(): whole = lax.all_gather(rows, 'dp', axis=0, tiled=True)]
    ppermute x0 -> x3, starting transfers between devices: none -> 3.8 us  [shards(): lax.ppermute(ring[-1], 'dp', [(dev, (dev + 1) % 4) for dev in range(4)])]
  transfers between devices with their start and end apart: 3 -> 5, of which waited for: 3 -> 5; matrix products, arithmetic and copies ran while one was open for 0% -> 0% of each run, Pallas kernels for 0% -> 0%
where the time goes in v1:
time: 299 us; the launch traced here: 298 us
  waiting for transfers between devices  170 us (57%)
  other arithmetic  56 us (19%)
  blocking collectives  37 us (12%)
  starting transfers between devices  12.5 us (4%)
  local copies, waits for them, and re-layouts  12.2 us (4%)
  matrix products  9.6 us (3%)
    ppermute x3, waiting for transfers between devices, shards(): lax.ppermute(ring[-1], 'dp', [(dev, (dev + 1) % 4) for dev in range(4)])  73.2 us
    all_to_all x1, waiting for transfers between devices, shards(): held = lax.all_to_all(gram.astype(jnp.bfloat16), 'member', 0, 0)  48.6 us
    all_to_all x1, waiting for transfers between devices, shards(): mixed = lax.all_to_all(mixed, 'member', 0, 0)  48.4 us
    unnamed x7, other arithmetic  43.5 us
    psum x1, blocking collectives, shards(): sums = lax.psum(jnp.stack(sums, axis=1), ('member', 'dp'))  37 us
    another operation x1, other arithmetic, shards(): jnp.stack([sum((mix[m, q] * held[q] for q in range(members))) for m in ra...  6.23 us
  transfers between devices with their start and end apart: 5, of which 5 were waited for; matrix products, arithmetic and copies ran while one was open for 0% of the time, Pallas kernels for 0%

profile of v1, /device:TPU:0, one launch (start us, length us, event | category | flops | bytes accessed | tf_op | source)
XLA Modules:
  0.0 298.3 jit_solution(5001556447284529945)
XLA Ops:
  0.6 3.0 %collective-permute-start = (bf16[512,1024]{1,0:T(8,128)(2,1)}, bf16[512,1024]{1,0:T(8,128)(2,1)S(1)}, u32[]{:S(2)}, u32[]{:S(2)}) collective-permute-start(bf16[512,1024]{1,0:T(8,128)(2,1)} %bitcast.135), channel_id=1, source_target_pairs={{0,1},{1,2},{2,3},{3,0},{4,5},{5,6},{6,7},{7,4},{8,9},{9,10},{10,1... | collective-permute-start | bytes 3145736 | tf_op jit(solution)/shard_map/ppermute | solution.py:32
  3.7 24.3 %collective-permute-done = bf16[512,1024]{1,0:T(8,128)(2,1)S(1)} collective-permute-done((bf16[512,1024]{1,0:T(8,128)(2,1)}, bf16[512,1024]{1,0:T(8,128)(2,1)S(1)}, u32[]{:S(2)}, u32[]{:S(2)}) %collective-permute-start) | collective-permute-done | bytes 1048608 | tf_op jit(solution)/shard_map/ppermute | solution.py:32
  28.8 24.4 %collective-permute-done.1 = bf16[512,1024]{1,0:T(8,128)(2,1)S(1)} collective-permute-done((bf16[512,1024]{1,0:T(8,128)(2,1)S(1)}, bf16[512,1024]{1,0:T(8,128)(2,1)S(1)}, u32[]{:S(2)}, u32[]{:S(2)}) %collective-permute-start.1) | collective-permute-done | bytes 1048608 | tf_op jit(solution)/shard_map/ppermute | solution.py:32
  53.2 24.5 %collective-permute-done.2 = bf16[512,1024]{1,0:T(8,128)(2,1)} collective-permute-done((bf16[512,1024]{1,0:T(8,128)(2,1)S(1)}, bf16[512,1024]{1,0:T(8,128)(2,1)}, u32[]{:S(2)}, u32[]{:S(2)}) %collective-permute-start.2) | collective-permute-done | bytes 1048608 | tf_op jit(solution)/shard_map/ppermute | solution.py:32
  77.7 1.3 constant_dynamic-update-slice_fusion.7
  79.2 1.3 constant_dynamic-update-slice_fusion.3
  81.5 1.3 fusion
  82.8 1.9 copy-done
  84.7 3.7 %convert_bitcast_fusion = bf16[8,512,256]{1,2,0:T(8,128)(2,1)} fusion(bf16[8,256,1024]{2,1,0:T(8,128)(2,1)S(1)} %bitcast.133, bf16[1,512,1024]{2,1,0:T(8,128)(2,1)S(1)} %copy-done.1, f32[1024]{0:T(1024)S(1)} %broadcast_multiply_fusion), kind=kOutput, calls=%fused_computation.12 | convolution fusion | flops 2150105088 | bytes 7344128 | tf_op jit(solution)/shard_map/rf,mcf->mrc/dot_general | solution.py:41
  88.5 4.5 %all-to-all-start = ((bf16[8,512,256]{1,2,0:T(8,128)(2,1)}), bf16[8,512,256]{1,2,0:T(8,128)(2,1)S(1)}, u32[]{:S(2)}, u32[]{:S(2)}) async-start(bf16[8,512,256]{1,2,0:T(8,128)(2,1)} %convert_bitcast_fusion), calls=%async_computation | async-start | bytes 4194304 | tf_op jit(solution)/shard_map/all_to_all | solution.py:42
  93.4 48.6 %all-to-all-done = bf16[8,512,256]{1,2,0:T(8,128)(2,1)S(1)} async-done(((bf16[8,512,256]{1,2,0:T(8,128)(2,1)}), bf16[8,512,256]{1,2,0:T(8,128)(2,1)S(1)}, u32[]{:S(2)}, u32[]{:S(2)}) %all-to-all-start) | async-done | bytes 2097184 | tf_op jit(solution)/shard_map/all_to_all | solution.py:42
  143.7 1.8 multiply_reduce_fusion
  145.6 37.0 %psum.7 = f32[8,4]{0,1:T(4,128)S(1)} all-reduce(f32[8,4]{0,1:T(4,128)S(1)} %pad_maximum_fusion), channel_id=1, replica_groups=mesh['member'=8,'dp'=4] {'member','dp'}, use_global_device_ids=true, to_apply=%region_5.6 | all-reduce | flops 32 | bytes 256 | tf_op jit(solution)/shard_map/psum | solution.py:47
  189.5 6.4 %fusion.8 = bf16[8,512,256]{1,2,0:T(8,128)(2,1)} fusion(f32[8,512,256]{1,2,0:T(8,128)S(1)} %convert_element_type.47, f32[]{:T(128)} %bitcast.34, f32[]{:T(128)} %bitcast.33, f32[]{:T(128)} %bitcast.32, f32[]{:T(128)} %bitcast.31, f32[]{:T(128)} %bitcast.30, f32[]{:T(128)} %bitcast.29, f32[]{:T(128)} %bitcast.28, f32[]{:T(128)} %bitcast.27), kind=kLoop, calls=%fused_computation.24 | loop fusion | flops 2097151 | bytes 4456480
  195.9 6.1 %fusion.9 = bf16[8,512,256]{1,2,0:T(8,128)(2,1)} fusion(bf16[8,512,256]{1,2,0:T(8,128)(2,1)} %fusion.8, f32[8,512,256]{1,2,0:T(8,128)S(1)} %convert_element_type.47, f32[]{:T(128)} %bitcast.42, f32[]{:T(128)} %bitcast.41, f32[]{:T(128)} %bitcast.40, f32[]{:T(128)} %bitcast.39, f32[]{:T(128)} %bitcast.38, f32[]{:T(128)} %bitcast.37, f32[]{:T(128)} %bitcast.36, ...), kind=kLoop, calls=%fused_computation.25 | loop fusion | flops 2097152 | bytes 4460544
  202.0 6.1 %fusion.10 = bf16[8,512,256]{1,2,0:T(8,128)(2,1)} fusion(bf16[8,512,256]{1,2,0:T(8,128)(2,1)} %fusion.9, f32[8,512,256]{1,2,0:T(8,128)S(1)} %convert_element_type.47, f32[]{:T(128)} %bitcast.50, f32[]{:T(128)} %bitcast.49, f32[]{:T(128)} %bitcast.48, f32[]{:T(128)} %bitcast.47, f32[]{:T(128)} %bitcast.46, f32[]{:T(128)} %bitcast.45, f32[]{:T(128)} %bitcast.44, ...), kind=kLoop, calls=%fused_computation.26 | loop fusion | flops 2097152 | bytes 4460544
  208.2 6.1 %fusion.11 = bf16[8,512,256]{1,2,0:T(8,128)(2,1)} fusion(bf16[8,512,256]{1,2,0:T(8,128)(2,1)} %fusion.10, f32[8,512,256]{1,2,0:T(8,128)S(1)} %convert_element_type.47, f32[]{:T(128)} %bitcast.58, f32[]{:T(128)} %bitcast.57, f32[]{:T(128)} %bitcast.56, f32[]{:T(128)} %bitcast.55, f32[]{:T(128)} %bitcast.54, f32[]{:T(128)} %bitcast.53, f32[]{:T(128)} %bitcast.52, ...), kind=kLoop, calls=%fused_computation.27 | loop fusion | flops 2097152 | bytes 4460544
  214.2 6.3 %fusion.12 = bf16[8,512,256]{1,2,0:T(8,128)(2,1)} fusion(bf16[8,512,256]{1,2,0:T(8,128)(2,1)} %fusion.11, f32[8,512,256]{1,2,0:T(8,128)S(1)} %convert_element_type.47, f32[]{:T(128)} %bitcast.66, f32[]{:T(128)} %bitcast.65, f32[]{:T(128)} %bitcast.64, f32[]{:T(128)} %bitcast.63, f32[]{:T(128)} %bitcast.62, f32[]{:T(128)} %bitcast.61, f32[]{:T(128)} %bitcast.60, ...), kind=kLoop, calls=%fused_computation.28 | loop fusion | flops 2097152 | bytes 4460544
  220.6 6.2 %fusion.13 = bf16[8,512,256]{1,2,0:T(8,128)(2,1)} fusion(bf16[8,512,256]{1,2,0:T(8,128)(2,1)} %fusion.12, f32[8,512,256]{1,2,0:T(8,128)S(1)} %convert_element_type.47, f32[]{:T(128)} %bitcast.74, f32[]{:T(128)} %bitcast.73, f32[]{:T(128)} %bitcast.72, f32[]{:T(128)} %bitcast.71, f32[]{:T(128)} %bitcast.70, f32[]{:T(128)} %bitcast.69, f32[]{:T(128)} %bitcast.68, ...), kind=kLoop, calls=%fused_computation.29 | loop fusion | flops 2097152 | bytes 4460544
  226.8 6.2 %fusion.14 = bf16[8,512,256]{1,2,0:T(8,128)(2,1)} fusion(bf16[8,512,256]{1,2,0:T(8,128)(2,1)} %fusion.13, f32[8,512,256]{1,2,0:T(8,128)S(1)} %convert_element_type.47, f32[]{:T(128)} %bitcast.82, f32[]{:T(128)} %bitcast.81, f32[]{:T(128)} %bitcast.80, f32[]{:T(128)} %bitcast.79, f32[]{:T(128)} %bitcast.78, f32[]{:T(128)} %bitcast.77, f32[]{:T(128)} %bitcast.76, ...), kind=kLoop, calls=%fused_computation.30 | loop fusion | flops 2097152 | bytes 4460544
  233.0 6.2 %fusion.15 = bf16[8,512,256]{1,2,0:T(8,128)(2,1)} fusion(bf16[8,512,256]{1,2,0:T(8,128)(2,1)} %fusion.14, f32[8,512,256]{1,2,0:T(8,128)S(1)} %convert_element_type.47, f32[]{:T(128)} %bitcast.90, f32[]{:T(128)} %bitcast.89, f32[]{:T(128)} %bitcast.88, f32[]{:T(128)} %bitcast.87, f32[]{:T(128)} %bitcast.86, f32[]{:T(128)} %bitcast.85, f32[]{:T(128)} %bitcast.84, ...), kind=kLoop, calls=%fused_computation.31 | loop fusion | flops 2097152 | bytes 4460544 | tf_op jit(solution)/shard_map/stack | solution.py:49
  239.2 4.2 %all-to-all-start.1 = ((bf16[8,512,256]{1,2,0:T(8,128)(2,1)}), bf16[8,512,256]{1,2,0:T(8,128)(2,1)S(1)}, u32[]{:S(2)}, u32[]{:S(2)}) async-start(bf16[8,512,256]{1,2,0:T(8,128)(2,1)} %fusion.15), calls=%async_computation.1 | async-start | bytes 4194304 | tf_op jit(solution)/shard_map/all_to_all | solution.py:52
  244.1 48.4 %all-to-all-done.1 = bf16[8,512,256]{1,2,0:T(8,128)(2,1)S(1)} async-done(((bf16[8,512,256]{1,2,0:T(8,128)(2,1)}), bf16[8,512,256]{1,2,0:T(8,128)(2,1)S(1)}, u32[]{:S(2)}, u32[]{:S(2)}) %all-to-all-start.1) | async-done | bytes 2097184 | tf_op jit(solution)/shard_map/all_to_all | solution.py:52
  292.5 5.9 %fusion.4 = f32[1,512,1024]{2,1,0:T(8,128)} fusion(bf16[8,512,256]{1,2,0:T(8,128)(2,1)S(1)} %all-to-all-done.1, bf16[8,256,1024]{2,1,0:T(8,128)(2,1)} %bitcast.134), kind=kOutput, calls=%fused_computation.11 | convolution fusion | flops 2148007936 | bytes 8388608 | tf_op jit(solution)/shard_map/jrc,jcf->rf/dot_general | solution.py:53
  (62 shorter events, 11.7 us)
Async XLA Ops:
  0.6 78.5 %copy-start.1 = (bf16[1,512,1024]{2,1,0:T(8,128)(2,1)S(1)}, bf16[1,512,1024]{2,1,0:T(8,128)(2,1)}, u32[]{:S(2)}) copy-start(bf16[1,512,1024]{2,1,0:T(8,128)(2,1)} %param.2) | copy-start | bytes 3145732
  0.6 27.4 %collective-permute-start = (bf16[512,1024]{1,0:T(8,128)(2,1)}, bf16[512,1024]{1,0:T(8,128)(2,1)S(1)}, u32[]{:S(2)}, u32[]{:S(2)}) collective-permute-start(bf16[512,1024]{1,0:T(8,128)(2,1)} %bitcast.135), channel_id=1, source_target_pairs={{0,1},{1,2},{2,3},{3,0},{4,5},{5,6},{6,7},{7,4},{8,9},{9,10},{10,1... | collective-permute-start | bytes 3145736 | tf_op jit(solution)/shard_map/ppermute | solution.py:32
  28.0 25.2 %collective-permute-start.1 = (bf16[512,1024]{1,0:T(8,128)(2,1)S(1)}, bf16[512,1024]{1,0:T(8,128)(2,1)S(1)}, u32[]{:S(2)}, u32[]{:S(2)}) collective-permute-start(bf16[512,1024]{1,0:T(8,128)(2,1)S(1)} %collective-permute-done), channel_id=1, source_target_pairs={{0,1},{1,2},{2,3},{3,0},{4,5},{5,6},{6,7},{7,4},{8,9},{9,10},{10,1... | collective-permute-start | bytes 3145736 | tf_op jit(solution)/shard_map/ppermute | solution.py:32
  53.2 24.5 %collective-permute-start.2 = (bf16[512,1024]{1,0:T(8,128)(2,1)S(1)}, bf16[512,1024]{1,0:T(8,128)(2,1)}, u32[]{:S(2)}, u32[]{:S(2)}) collective-permute-start(bf16[512,1024]{1,0:T(8,128)(2,1)S(1)} %collective-permute-done.1), channel_id=1, source_target_pairs={{0,1},{1,2},{2,3},{3,0},{4,5},{5,6},{6,7},{7,4},{8,9},{9,10},{10,1... | collective-permute-start | bytes 3145736 | tf_op jit(solution)/shard_map/ppermute | solution.py:32
  82.8 1.9 copy-start
  88.5 53.5 %all-to-all-start = ((bf16[8,512,256]{1,2,0:T(8,128)(2,1)}), bf16[8,512,256]{1,2,0:T(8,128)(2,1)S(1)}, u32[]{:S(2)}, u32[]{:S(2)}) async-start(bf16[8,512,256]{1,2,0:T(8,128)(2,1)} %convert_bitcast_fusion), calls=%async_computation | async-start | bytes 4194304 | tf_op jit(solution)/shard_map/all_to_all | solution.py:42
  143.7 40.5 %copy-start.2 = (f32[8,3]{0,1:T(4,128)S(1)}, f32[8,3]{0,1:T(4,128)}, u32[]{:S(2)}) copy-start(f32[8,3]{0,1:T(4,128)} %param.3) | copy-start | bytes 292
  239.2 53.3 %all-to-all-start.1 = ((bf16[8,512,256]{1,2,0:T(8,128)(2,1)}), bf16[8,512,256]{1,2,0:T(8,128)(2,1)S(1)}, u32[]{:S(2)}, u32[]{:S(2)}) async-start(bf16[8,512,256]{1,2,0:T(8,128)(2,1)} %fusion.15), calls=%async_computation.1 | async-start | bytes 4194304 | tf_op jit(solution)/shard_map/all_to_all | solution.py:52
